TPU v7x, 32 devices: a whole 2x2x4 slice. The times are simulated.
32 devices in a mesh: groups: 2 (over x), seq: 16 (over z, y, core).
Axes of the slice: x: 2, y: 2, z: 4, core: 2. Of those that a mesh axis runs over, the one named last changes fastest.
Arguments:
- query_in: bfloat16 [4096, 4096], P(('groups', 'seq')), parts along dimension 0, may hold values from -6 to 6
- key_in: bfloat16 [4096, 4096], P(('groups', 'seq')), parts along dimension 0, may hold values from -6 to 6
- value_in: bfloat16 [4096, 4096], P(('groups', 'seq')), parts along dimension 0, may hold values from -6 to 6
- long_filter: bfloat16 [2048, 4096], P('seq'), may hold values from -0.4 to 0.4
- short_weight: float32 [3, 3, 4096], replicated, may hold values from -3 to 3
- skip_gain: float32 [4096], replicated, may hold values from 0.5 to 1.5
Outputs:
- gated_out: bfloat16 [4096, 4096], P(('groups', 'seq')), parts along dimension 0
There are 2 independent parts, one for each index of `groups`. A program takes and returns all parts, laid end to end along the dimension named above; an argument that names none is the same for every part. Nothing has to cross between parts.
All inputs are finite; a program needn't handle non-finite values.
Results may differ from a plain program's by a relative error of at most 0.0052.
Values may be sent and summed in bfloat16 or wider, within the bound.
No kernel may reach another device: no remote copies, remote signals or barrier semaphores. Data moves between devices by JAX's collectives and lax.ppermute only.
A program may use at most 128 MiB of HBM per device.

v0:
```python
import math
import jax
import jax.numpy as jnp
from jax import lax
from jax.sharding import PartitionSpec as P

PRECISE = lax.Precision.HIGHEST


def from_behind(value, axis, steps):
    count = lax.axis_size(axis)
    initial, last = (max(0, -steps), min(count, count - steps))
    return lax.ppermute(value, axis, [(source, source + steps) for source in range(initial, last)])


def featurize(own_rows, earlier, taps_weight):
    rim_rows = earlier.shape[0]
    row_count = own_rows.shape[0]
    extended = jnp.concatenate([earlier, own_rows], axis=0).astype(jnp.float32)
    result = jnp.zeros(own_rows.shape, jnp.float32)
    for offset in range(rim_rows + 1):
        result = (
            result
            + taps_weight[offset] * extended[rim_rows - offset : rim_rows - offset + row_count]
        )
    return result


def phase_pair(left_index, right_index, modulus):
    product_index = left_index[:, None] * right_index[None, :] % modulus
    angle = product_index.astype(jnp.float32) * (2.0 * math.pi / modulus)
    return (jnp.cos(angle), jnp.sin(angle))


def block_forward(real_blocks):
    blocks = real_blocks.shape[0]
    flat_values = real_blocks.reshape(blocks, -1)
    cosine_table, sine_table = phase_pair(
        jnp.arange(2 * blocks, dtype=jnp.int32), jnp.arange(blocks, dtype=jnp.int32), 2 * blocks
    )
    joint_table = jnp.concatenate([cosine_table, -sine_table], axis=0)
    stacked = jnp.dot(joint_table, flat_values, precision=PRECISE)
    return stacked.reshape((2, 2 * blocks) + real_blocks.shape[1:])


def apply_twiddle(stacked, freq_index, row_index, modulus, direction):
    cosine_table, sine_table = phase_pair(freq_index, row_index, modulus)
    cosine_table = cosine_table[:, :, None]
    sine_table = direction * sine_table[:, :, None]
    out_real = stacked[0] * cosine_table + stacked[1] * sine_table
    out_imaginary = stacked[1] * cosine_table - stacked[0] * sine_table
    return jnp.stack([out_real, out_imaginary])


def row_transform(stacked, direction):
    length = stacked.shape[2]
    row_index = jnp.arange(length, dtype=jnp.int32)
    cosine_table, sine_table = phase_pair(row_index, row_index, length)
    sine_table = direction * sine_table
    upper_table = jnp.stack([cosine_table, sine_table], axis=1)
    lower_table = jnp.stack([-sine_table, cosine_table], axis=1)
    full_table = jnp.stack([upper_table, lower_table])
    return jnp.einsum("ymxn,xknc->ykmc", full_table, stacked, precision=PRECISE)


def block_inverse(stacked, factor):
    double_count = stacked.shape[1]
    blocks = double_count // 2
    cosine_table, sine_table = phase_pair(
        jnp.arange(blocks, dtype=jnp.int32), jnp.arange(double_count, dtype=jnp.int32), double_count
    )
    joint_table = jnp.concatenate([cosine_table, -sine_table], axis=1)
    flat_values = stacked.reshape(2 * double_count, -1)
    result = jnp.dot(joint_table, flat_values, precision=PRECISE) * factor
    return result.reshape((blocks,) + stacked.shape[2:])


def spectral_product(stacked, width):
    spectra = row_transform(stacked, 1.0)
    data_real = spectra[0, ..., :width]
    kernel_real = spectra[0, ..., width:]
    data_imaginary = spectra[1, ..., :width]
    kernel_imaginary = spectra[1, ..., width:]
    joint = jnp.stack(
        [
            data_real * kernel_real - data_imaginary * kernel_imaginary,
            data_real * kernel_imaginary + data_imaginary * kernel_real,
        ]
    )
    return row_transform(joint, -1.0)


def along_rows(product, long_filter):
    blocks = lax.axis_size("seq")
    device_index = lax.axis_index("seq")
    row_count, channels = product.shape
    row_share = row_count // blocks
    full_length = 2 * blocks * row_count
    data_parts, kernel_parts = (
        lax.all_to_all(
            product.reshape(1, row_count, channels), "seq", split_axis=1, concat_axis=0, tiled=True
        ),
        lax.all_to_all(
            long_filter.reshape(1, row_count, channels),
            "seq",
            split_axis=1,
            concat_axis=0,
            tiled=True,
        ),
    )
    joined = jnp.concatenate([data_parts, kernel_parts], axis=2).astype(jnp.float32)
    freq_all = jnp.arange(2 * blocks, dtype=jnp.int32)
    local_rows = device_index * row_share + jnp.arange(row_share, dtype=jnp.int32)
    spectra = apply_twiddle(block_forward(joined), freq_all, local_rows, full_length, 1.0)
    spectra = lax.all_to_all(spectra, "seq", split_axis=1, concat_axis=2, tiled=True)
    joint = spectral_product(spectra, channels)
    own_freq = device_index * 2 + jnp.arange(2, dtype=jnp.int32)
    whole_rows = jnp.arange(row_count, dtype=jnp.int32)
    joint = apply_twiddle(joint, own_freq, whole_rows, full_length, -1.0)
    joint = lax.all_to_all(
        joint.astype(jnp.bfloat16), "seq", split_axis=2, concat_axis=1, tiled=True
    ).astype(joint.dtype)
    convolved = block_inverse(joint, 1.0 / full_length).astype(jnp.bfloat16)
    convolved = lax.all_to_all(convolved, "seq", split_axis=0, concat_axis=1, tiled=True)
    return convolved.reshape(row_count, channels)


def on_device(query_in, key_in, value_in, long_filter, short_weight, skip_gain):
    rim_rows = short_weight.shape[1] - 1
    last_rows = jnp.stack([query_in[-rim_rows:], key_in[-rim_rows:], value_in[-rim_rows:]])
    earlier = from_behind(last_rows, "seq", 1)
    q_short = featurize(query_in, earlier[0], short_weight[0])
    k_short = featurize(key_in, earlier[1], short_weight[1])
    v_short = featurize(value_in, earlier[2], short_weight[2])
    product = (k_short * v_short).astype(jnp.bfloat16)
    product_wide = lax.optimization_barrier(product).astype(jnp.float32)
    convolved = along_rows(product, long_filter)
    gated_out = q_short * (convolved.astype(jnp.float32) + skip_gain * product_wide)
    return gated_out.astype(jnp.bfloat16)


def solution(mesh):
    placed = (
        P(("groups", "seq"), None),
        P(("groups", "seq"), None),
        P(("groups", "seq"), None),
        P("seq", None),
        P(),
        P(),
    )
    return jax.shard_map(
        on_device, mesh=mesh, in_specs=placed, out_specs=P(("groups", "seq"), None), check_vma=False
    )
```

profile of v0, /device:TPU:9, one launch (start us, length us, event | category | flops | bytes accessed | tf_op | source)
XLA Modules:
  0.0 698.6 jit_solution(10720077850557271215)
XLA Ops:
  0.0 0.9 slice_bitcast_fusion.5
  0.9 0.9 slice_bitcast_fusion.3
  1.9 3.7 collective-permute-start
  5.6 3.6 copy.66
  9.2 0.5 broadcast.416
  9.7 7.0 %reduce = bf16[128,4096]{1,0:T(8,128)(2,1)S(1)} reduce(bf16[128,1,4096]{2,1,0:T(2,128)(2,1)S(1)} %bitcast.152, bf16[]{:T(256)} %broadcast.416), dimensions={1}, to_apply=%bitcast.138.reduce_sub_computation | reduce | bytes 2097154
  16.8 1.9 reshape.316
  18.7 5.7 all-to-all-start.1
  24.6 0.3 maximum_convert_fusion.1
  24.9 0.3 maximum_convert_fusion.2
  25.2 1.3 fusion.18
  26.5 2.4 copy.67
  28.9 8.0 %reduce.1 = bf16[128,4096]{1,0:T(8,128)(2,1)} reduce(bf16[128,1,4096]{2,1,0:T(2,128)(2,1)S(1)} %bitcast.154, bf16[]{:T(256)} %broadcast.416), dimensions={1}, to_apply=%bitcast.139.reduce_sub_computation | reduce | bytes 2097154
  36.9 2.9 reshape.318
  39.8 9.3 %all-to-all-done.1 = bf16[16,2,16384]{2,1,0:T(2,128)(2,1)} async-done(((bf16[16,2,16384]{2,1,0:T(2,128)(2,1)}), bf16[16,2,16384]{2,1,0:T(2,128)(2,1)}, u32[]{:S(2)}, u32[]{:S(2)}) %all-to-all-start.1) | async-done | bytes 1048608 | tf_op jit(solution)/shard_map/all_to_all | solution.py:103
  49.2 5.3 all-to-all-start
  54.6 4.3 reshape.317
  59.0 2.1 copy.64
  61.1 18.2 %all-to-all-done = bf16[16,2,16384]{2,1,0:T(2,128)(2,1)} async-done(((bf16[16,2,16384]{2,1,0:T(2,128)(2,1)}), bf16[16,2,16384]{2,1,0:T(2,128)(2,1)}, u32[]{:S(2)}, u32[]{:S(2)}) %all-to-all-start) | async-done | bytes 1048608 | tf_op jit(solution)/shard_map/all_to_all | solution.py:100
  79.3 4.3 reshape.319
  83.6 1.1 copy.65
  84.7 1.4 pad_maximum_fusion.2
  86.1 1.2 copy.46
  87.3 6.8 fusion.59
  94.1 6.5 fusion.81
  100.6 8.2 %copy.48 = f32[4,8,8,8192]{3,2,1,0:T(8,128)S(1)} copy(f32[4,8,8,8192]{3,1,2,0:T(8,128)} %bitcast.145) | data formatting | bytes 16777216
  108.8 8.2 %copy.47 = f32[4,8,8,8192]{3,2,1,0:T(8,128)S(1)} copy(f32[4,8,8,8192]{3,1,2,0:T(8,128)} %bitcast.144) | data formatting | bytes 16777216
  117.1 6.9 fusion.8
  124.0 11.5 %pad_maximum_fusion = f32[2,32,8,8192]{3,2,0,1:T(8,128)} fusion(f32[1,32,8,8192]{3,2,0,1:T(8,128)} %get-tuple-element.6, f32[1,32,8,8192]{3,2,0,1:T(8,128)} %get-tuple-element.5), kind=kLoop, calls=%fused_computation.2 | loop fusion | flops 4194304 | bytes 33554432 | tf_op jit(solution)/shard_map/stack | solution.py:52
  135.5 5.5 all-to-all-start.2
  142.0 358.8 %all-to-all-done.2 = f32[2,32,8,8192]{3,2,0,1:T(8,128)} async-done(((f32[2,32,8,8192]{3,2,0,1:T(8,128)}), f32[2,32,8,8192]{3,2,0,1:T(8,128)}, u32[]{:S(2)}, u32[]{:S(2)}) %all-to-all-start.2) | async-done | bytes 16777248 | tf_op jit(solution)/shard_map/all_to_all | solution.py:115
  500.8 30.7 %fusion.3 = f32[2,2,128,8192]{2,3,0,1:T(8,128)S(1)} fusion(f32[1,128,2,128]{3,1,2,0:T(8,128)S(1)} %get-tuple-element.24, f32[1,128,2,128]{3,1,2,0:T(8,128)S(1)} %get-tuple-element.25, f32[2,2,16,8,8192]{4,3,0,1,2:T(8,128)} %bitcast.23), kind=kOutput, calls=%fused_computation.6 | convolution fusion | flops 12884967424 | bytes 33816576 | tf_op jit(solution)/shard_map/ymxn,xknc->ykmc/dot_general | solution.py:63
  531.5 1.1 multiply_subtract_fusion
  532.6 6.7 fusion.15
  539.3 1.1 add_convert_fusion
  540.4 2.4 pad_maximum_fusion.1
  542.8 11.2 %copy.34 = bf16[2,2,128,4096]{3,0,1,2:T(2,128)(2,1)} copy(bf16[2,2,128,4096]{2,3,0,1:T(8,128)(2,1)} %pad_maximum_fusion.1) | data formatting | bytes 8388608 | tf_op jit(solution)/shard_map/stack | solution.py:52
  554.0 7.4 %all-to-all-start.3 = ((bf16[2,2,128,4096]{3,0,1,2:T(2,128)(2,1)}), bf16[2,2,128,4096]{3,0,1,2:T(2,128)(2,1)}, u32[]{:S(2)}, u32[]{:S(2)}) async-start(bf16[2,2,128,4096]{3,0,1,2:T(2,128)(2,1)} %copy.34), calls=%async_computation.3 | async-start | bytes 8388608 | tf_op jit(solution)/shard_map/all_to_all | solution.py:120
  561.5 90.1 %all-to-all-done.3 = bf16[2,2,128,4096]{3,0,1,2:T(2,128)(2,1)} async-done(((bf16[2,2,128,4096]{3,0,1,2:T(2,128)(2,1)}), bf16[2,2,128,4096]{3,0,1,2:T(2,128)(2,1)}, u32[]{:S(2)}, u32[]{:S(2)}) %all-to-all-start.3) | async-done | bytes 4194336 | tf_op jit(solution)/shard_map/all_to_all | solution.py:120
  651.6 5.1 copy.63
  656.7 0.5 copy.36
  657.2 2.6 copy.49
  659.8 1.8 fusion
  661.6 1.5 copy.50
  663.2 7.1 %all-to-all-start.4 = ((bf16[16,8,4096]{2,1,0:T(8,128)(2,1)}), bf16[16,8,4096]{2,1,0:T(8,128)(2,1)}, u32[]{:S(2)}, u32[]{:S(2)}) async-start(bf16[16,8,4096]{2,1,0:T(8,128)(2,1)} %bitcast.63), calls=%async_computation.4 | async-start | bytes 2097152 | tf_op jit(solution)/shard_map/all_to_all | solution.py:124
  670.3 1.5 maximum_convert_fusion
  671.8 23.4 %all-to-all-done.4 = bf16[16,8,4096]{2,1,0:T(8,128)(2,1)} async-done(((bf16[16,8,4096]{2,1,0:T(8,128)(2,1)}), bf16[16,8,4096]{2,1,0:T(8,128)(2,1)}, u32[]{:S(2)}, u32[]{:S(2)}) %all-to-all-start.4) | async-done | bytes 1048608 | tf_op jit(solution)/shard_map/all_to_all | solution.py:124
  695.2 3.2 fusion.24
  (22 shorter events, 1.4 us)
Async XLA Ops:
  1.9 22.6 %collective-permute-start = (bf16[3,2,4096]{2,1,0:T(2,128)(2,1)S(1)}, bf16[3,2,4096]{2,1,0:T(2,128)(2,1)S(1)}, u32[]{:S(2)}, u32[]{:S(2)}) collective-permute-start(bf16[3,2,4096]{2,1,0:T(2,128)(2,1)S(1)} %pad_maximum_fusion.7), channel_id=1, source_target_pairs={{0,1},{1,2},{2,3},{3,4},{4,5},{5,6},{6,7},{7,8},{8,9},{9,10},{10,1... | collective-permute-start | bytes 147464 | tf_op jit(solution)/shard_map/ppermute | solution.py:13
  9.2 15.2 %copy-start.2 = (f32[3,3,4096]{2,1,0:T(4,128)S(1)}, f32[3,3,4096]{2,1,0:T(4,128)}, u32[]{:S(2)}) copy-start(f32[3,3,4096]{2,1,0:T(4,128)} %param.10) | copy-start | bytes 442372
  16.7 7.8 %copy-start = (bf16[128,4096]{1,0:T(8,128)(2,1)S(1)}, bf16[128,4096]{1,0:T(8,128)(2,1)}, u32[]{:S(2)}) copy-start(bf16[128,4096]{1,0:T(8,128)(2,1)} %param.7) | copy-start | bytes 3145732
  16.8 8.1 %copy-start.1 = (bf16[128,4096]{1,0:T(8,128)(2,1)S(1)}, bf16[128,4096]{1,0:T(8,128)(2,1)}, u32[]{:S(2)}) copy-start(bf16[128,4096]{1,0:T(8,128)(2,1)} %param.8) | copy-start | bytes 3145732
  18.7 30.5 %all-to-all-start.1 = ((bf16[16,2,16384]{2,1,0:T(2,128)(2,1)}), bf16[16,2,16384]{2,1,0:T(2,128)(2,1)}, u32[]{:S(2)}, u32[]{:S(2)}) async-start(bf16[16,2,16384]{2,1,0:T(2,128)(2,1)} %reshape.316), calls=%async_computation.1 | async-start | bytes 2097152 | tf_op jit(solution)/shard_map/all_to_all | solution.py:103
  49.2 30.1 %all-to-all-start = ((bf16[16,2,16384]{2,1,0:T(2,128)(2,1)}), bf16[16,2,16384]{2,1,0:T(2,128)(2,1)}, u32[]{:S(2)}, u32[]{:S(2)}) async-start(bf16[16,2,16384]{2,1,0:T(2,128)(2,1)} %reshape.318), calls=%async_computation | async-start | bytes 2097152 | tf_op jit(solution)/shard_map/all_to_all | solution.py:100
  135.5 365.3 %all-to-all-start.2 = ((f32[2,32,8,8192]{3,2,0,1:T(8,128)}), f32[2,32,8,8192]{3,2,0,1:T(8,128)}, u32[]{:S(2)}, u32[]{:S(2)}) async-start(f32[2,32,8,8192]{3,2,0,1:T(8,128)} %pad_maximum_fusion), calls=%async_computation.2 | async-start | bytes 33554432 | tf_op jit(solution)/shard_map/all_to_all | solution.py:115
  554.0 97.6 %all-to-all-start.3 = ((bf16[2,2,128,4096]{3,0,1,2:T(2,128)(2,1)}), bf16[2,2,128,4096]{3,0,1,2:T(2,128)(2,1)}, u32[]{:S(2)}, u32[]{:S(2)}) async-start(bf16[2,2,128,4096]{3,0,1,2:T(2,128)(2,1)} %copy.34), calls=%async_computation.3 | async-start | bytes 8388608 | tf_op jit(solution)/shard_map/all_to_all | solution.py:120
  661.6 33.6 %copy-start.3 = (f32[4096]{0:T(1024)S(1)}, f32[4096]{0:T(1024)}, u32[]{:S(2)}) copy-start(f32[4096]{0:T(1024)} %param.11) | copy-start | bytes 49156
  663.2 32.0 %all-to-all-start.4 = ((bf16[16,8,4096]{2,1,0:T(8,128)(2,1)}), bf16[16,8,4096]{2,1,0:T(8,128)(2,1)}, u32[]{:S(2)}, u32[]{:S(2)}) async-start(bf16[16,8,4096]{2,1,0:T(8,128)(2,1)} %bitcast.63), calls=%async_computation.4 | async-start | bytes 2097152 | tf_op jit(solution)/shard_map/all_to_all | solution.py:124
where the time goes:
time: 707 us; the launch traced here: 699 us
  waiting for transfers between devices  500 us (71%)
  local copies, waits for them, and re-layouts  70.2 us (10%)
  other arithmetic  47.2 us (7%)
  matrix products  46.1 us (7%)
  starting transfers between devices  34.7 us (5%)
    all_to_all x1, waiting for transfers between devices, along_rows(): lax.all_to_all(spectra, 'seq', split_axis=1, concat_axis=2, tiled=True)  359 us
    all_to_all x1, waiting for transfers between devices, along_rows(): lax.all_to_all(joint.astype(jnp.bfloat16), 'seq', split_axis=2, concat_ax...  90.1 us
    unnamed x20, local copies, waits for them, and re-layouts  39.1 us
    dot_general x2, matrix products, row_transform(): return jnp.einsum('ymxn,xknc->ykmc', full_table, stacked, precision=PRECISE)  37.4 us
    all_to_all x1, waiting for transfers between devices, along_rows(): lax.all_to_all(convolved, 'seq', split_axis=0, concat_axis=1, tiled=True)  23.4 us
    all_to_all x1, waiting for transfers between devices, along_rows(): lax.all_to_all(product.reshape(1, row_count, channels), 'seq', split_axis...  18.2 us
    unnamed x2, other arithmetic  15 us
  transfers between devices with their start and end apart: 6, of which 5 were waited for; matrix products, arithmetic and copies ran while one was open for 5% of the time, Pallas kernels for 0%

commit v1 on v0

--- a/solution.py
+++ b/solution.py
@@ -100,12 +100,18 @@
         lax.all_to_all(
             product.reshape(1, row_count, channels), "seq", split_axis=1, concat_axis=0, tiled=True
         ),
-        lax.all_to_all(
-            long_filter.reshape(1, row_count, channels),
-            "seq",
-            split_axis=1,
-            concat_axis=0,
-            tiled=True,
+        jnp.concatenate(
+            lax.all_to_all(
+                jnp.stack(
+                    jnp.split(
+                        long_filter.reshape(1, row_count, channels), lax.axis_size("seq"), axis=1
+                    )
+                ),
+                "seq",
+                0,
+                0,
+            ),
+            axis=0,
         ),
     )
     joined = jnp.concatenate([data_parts, kernel_parts], axis=2).astype(jnp.float32)

time: 707 us -> 728 us (1.030)
  local copies, waits for them, and re-layouts: 70.2 us -> 84.3 us
  waiting for transfers between devices: 500 us -> 511 us
    unnamed x20 -> x30, local copies, waits for them, and re-layouts: 39.1 us -> 53.8 us
    all_to_all x1, waiting for transfers between devices: 9.34 us -> 18.3 us  [along_rows(): lax.all_to_all(jnp.stack(jnp.split(long_filter.reshape(1, row_count, chan...]
    unnamed x2 -> x1, other arithmetic: 15 us -> 8 us
where the time goes in v1:
time: 728 us; the launch traced here: 718 us
  waiting for transfers between devices  511 us (70%)
  local copies, waits for them, and re-layouts  84.3 us (12%)
  matrix products  46.1 us (6%)
  other arithmetic  41.8 us (6%)
  starting transfers between devices  33.9 us (5%)
    all_to_all x1, waiting for transfers between devices, along_rows(): lax.all_to_all(spectra, 'seq', split_axis=1, concat_axis=2, tiled=True)  359 us
    all_to_all x1, waiting for transfers between devices, along_rows(): lax.all_to_all(joint.astype(jnp.bfloat16), 'seq', split_axis=2, concat_ax...  90.1 us
    unnamed x30, local copies, waits for them, and re-layouts  53.8 us
    dot_general x2, matrix products, row_transform(): return jnp.einsum('ymxn,xknc->ykmc', full_table, stacked, precision=PRECISE)  37.4 us
    all_to_all x1, waiting for transfers between devices, along_rows(): lax.all_to_all(convolved, 'seq', split_axis=0, concat_axis=1, tiled=True)  23.4 us
    all_to_all x1, waiting for transfers between devices, along_rows(): lax.all_to_all(product.reshape(1, row_count, channels), 'seq', split_axis...  20.3 us
    all_to_all x1, waiting for transfers between devices, along_rows(): lax.all_to_all(jnp.stack(jnp.split(long_filter.reshape(1, row_count, chan...  18.3 us
  transfers between devices with their start and end apart: 6, of which 5 were waited for; matrix products, arithmetic and copies ran while one was open for 5% of the time, Pallas kernels for 0%

profile of v1, /device:TPU:9, one launch (start us, length us, event | category | flops | bytes accessed | tf_op | source)
XLA Modules:
  0.0 717.7 jit_solution(12662536486576392163)
XLA Ops:
  2.0 3.7 collective-permute-start
  5.7 1.5 fusion.52
  7.1 1.5 fusion.51
  8.6 1.5 fusion.50
  10.1 1.5 fusion.49
  11.6 1.5 fusion.48
  13.0 1.5 fusion.47
  14.5 1.5 fusion.46
  16.0 1.5 fusion.45
  17.5 1.5 fusion.44
  18.9 1.5 fusion.43
  20.4 1.5 fusion.42
  21.9 1.5 fusion.41
  24.6 1.5 fusion.40
  26.1 1.5 maximum_convert_fusion.1
  29.3 2.4 copy.87
  32.2 8.0 %reduce = bf16[128,4096]{1,0:T(8,128)(2,1)} reduce(bf16[128,1,4096]{2,1,0:T(2,128)(2,1)S(1)} %bitcast.209, bf16[]{:T(256)} %broadcast.416), dimensions={1}, to_apply=%bitcast.197.reduce_sub_computation | reduce | bytes 2097154
  40.2 2.9 reshape.317
  43.2 5.4 all-to-all-start
  48.6 1.5 fusion.39
  53.0 20.3 %all-to-all-done = bf16[16,2,16384]{2,1,0:T(2,128)(2,1)S(1)} async-done(((bf16[16,2,16384]{2,1,0:T(2,128)(2,1)}), bf16[16,2,16384]{2,1,0:T(2,128)(2,1)S(1)}, u32[]{:S(2)}, u32[]{:S(2)}) %all-to-all-start) | async-done | bytes 1048608 | tf_op jit(solution)/shard_map/all_to_all | solution.py:100
  73.3 5.0 all-to-all-start.1
  78.4 4.3 reshape.318
  82.8 2.1 copy.86
  84.9 18.3 %all-to-all-done.1 = bf16[16,1,8,4096]{3,2,1,0:T(8,128)(2,1)} async-done(((bf16[16,1,8,4096]{3,2,1,0:T(8,128)(2,1)}), bf16[16,1,8,4096]{3,2,1,0:T(8,128)(2,1)}, u32[]{:S(2)}, u32[]{:S(2)}) %all-to-all-start.1) | async-done | bytes 1048608 | tf_op jit(solution)/shard_map/all_to_all | solution.py:104
  103.2 1.7 pad_maximum_fusion.2
  106.1 6.8 fusion.75
  112.9 6.6 fusion.97
  119.6 8.2 %copy.72 = f32[4,8,8,8192]{3,2,1,0:T(8,128)S(1)} copy(f32[4,8,8,8192]{3,1,2,0:T(8,128)} %bitcast.203) | data formatting | bytes 16777216
  127.8 8.2 %copy.71 = f32[4,8,8,8192]{3,2,1,0:T(8,128)S(1)} copy(f32[4,8,8,8192]{3,1,2,0:T(8,128)} %bitcast.202) | data formatting | bytes 16777216
  136.1 6.9 fusion.8
  143.0 11.5 %pad_maximum_fusion = f32[2,32,8,8192]{3,2,0,1:T(8,128)} fusion(f32[1,32,8,8192]{3,2,0,1:T(8,128)} %get-tuple-element.6, f32[1,32,8,8192]{3,2,0,1:T(8,128)} %get-tuple-element.5), kind=kLoop, calls=%fused_computation.2 | loop fusion | flops 4194304 | bytes 33554432 | tf_op jit(solution)/shard_map/stack | solution.py:52
  154.5 5.3 all-to-all-start.2
  160.8 358.8 %all-to-all-done.2 = f32[2,32,8,8192]{3,2,0,1:T(8,128)} async-done(((f32[2,32,8,8192]{3,2,0,1:T(8,128)}), f32[2,32,8,8192]{3,2,0,1:T(8,128)}, u32[]{:S(2)}, u32[]{:S(2)}) %all-to-all-start.2) | async-done | bytes 16777248 | tf_op jit(solution)/shard_map/all_to_all | solution.py:121
  519.6 30.7 %fusion.3 = f32[2,2,128,8192]{2,3,0,1:T(8,128)S(1)} fusion(f32[1,128,2,128]{3,1,2,0:T(8,128)S(1)} %get-tuple-element.24, f32[1,128,2,128]{3,1,2,0:T(8,128)S(1)} %get-tuple-element.25, f32[2,2,16,8,8192]{4,3,0,1,2:T(8,128)} %bitcast.40), kind=kOutput, calls=%fused_computation.6 | convolution fusion | flops 12884967424 | bytes 33816576 | tf_op jit(solution)/shard_map/ymxn,xknc->ykmc/dot_general | solution.py:63
  551.4 6.7 fusion.15
  559.2 2.4 pad_maximum_fusion.1
  561.6 11.2 %copy.59 = bf16[2,2,128,4096]{3,0,1,2:T(2,128)(2,1)} copy(bf16[2,2,128,4096]{2,3,0,1:T(8,128)(2,1)} %pad_maximum_fusion.1) | data formatting | bytes 8388608 | tf_op jit(solution)/shard_map/stack | solution.py:52
  572.9 7.5 %all-to-all-start.3 = ((bf16[2,2,128,4096]{3,0,1,2:T(2,128)(2,1)}), bf16[2,2,128,4096]{3,0,1,2:T(2,128)(2,1)}, u32[]{:S(2)}, u32[]{:S(2)}) async-start(bf16[2,2,128,4096]{3,0,1,2:T(2,128)(2,1)} %copy.59), calls=%async_computation.3 | async-start | bytes 8388608 | tf_op jit(solution)/shard_map/all_to_all | solution.py:126
  580.4 90.1 %all-to-all-done.3 = bf16[2,2,128,4096]{3,0,1,2:T(2,128)(2,1)} async-done(((bf16[2,2,128,4096]{3,0,1,2:T(2,128)(2,1)}), bf16[2,2,128,4096]{3,0,1,2:T(2,128)(2,1)}, u32[]{:S(2)}, u32[]{:S(2)}) %all-to-all-start.3) | async-done | bytes 4194336 | tf_op jit(solution)/shard_map/all_to_all | solution.py:126
  670.5 5.1 copy.85
  676.1 2.6 copy.73
  678.7 1.8 fusion
  680.5 1.5 copy.74
  682.1 7.1 all-to-all-start.4
  689.1 1.5 maximum_convert_fusion
  690.7 23.4 %all-to-all-done.4 = bf16[16,8,4096]{2,1,0:T(8,128)(2,1)} async-done(((bf16[16,8,4096]{2,1,0:T(8,128)(2,1)}), bf16[16,8,4096]{2,1,0:T(8,128)(2,1)}, u32[]{:S(2)}, u32[]{:S(2)}) %all-to-all-start.4) | async-done | bytes 1048608 | tf_op jit(solution)/shard_map/all_to_all | solution.py:130
  714.1 3.2 fusion.24
  (31 shorter events, 13.4 us)
Async XLA Ops:
  0.0 27.7 %copy-start.1 = (bf16[128,4096]{1,0:T(8,128)(2,1)S(1)}, bf16[128,4096]{1,0:T(8,128)(2,1)}, u32[]{:S(2)}) copy-start(bf16[128,4096]{1,0:T(8,128)(2,1)} %param.8) | copy-start | bytes 3145732
  2.0 24.1 %collective-permute-start = (bf16[3,2,4096]{2,1,0:T(2,128)(2,1)S(1)}, bf16[3,2,4096]{2,1,0:T(2,128)(2,1)S(1)}, u32[]{:S(2)}, u32[]{:S(2)}) collective-permute-start(bf16[3,2,4096]{2,1,0:T(2,128)(2,1)S(1)} %pad_maximum_fusion.7), channel_id=1, source_target_pairs={{0,1},{1,2},{2,3},{3,4},{4,5},{5,6},{6,7},{7,8},{8,9},{9,10},{10,1... | collective-permute-start | bytes 147464 | tf_op jit(solution)/shard_map/ppermute | solution.py:13
  43.2 30.1 %all-to-all-start = ((bf16[16,2,16384]{2,1,0:T(2,128)(2,1)}), bf16[16,2,16384]{2,1,0:T(2,128)(2,1)S(1)}, u32[]{:S(2)}, u32[]{:S(2)}) async-start(bf16[16,2,16384]{2,1,0:T(2,128)(2,1)} %reshape.317), calls=%async_computation | async-start | bytes 2097152 | tf_op jit(solution)/shard_map/all_to_all | solution.py:100
  73.3 5.0 copy-start
  73.3 29.9 %all-to-all-start.1 = ((bf16[16,1,8,4096]{3,2,1,0:T(8,128)(2,1)}), bf16[16,1,8,4096]{3,2,1,0:T(8,128)(2,1)}, u32[]{:S(2)}, u32[]{:S(2)}) async-start(bf16[16,1,8,4096]{3,2,1,0:T(8,128)(2,1)} %fusion.37), calls=%async_computation.1 | async-start | bytes 2097152 | tf_op jit(solution)/shard_map/all_to_all | solution.py:104
  154.5 365.1 %all-to-all-start.2 = ((f32[2,32,8,8192]{3,2,0,1:T(8,128)}), f32[2,32,8,8192]{3,2,0,1:T(8,128)}, u32[]{:S(2)}, u32[]{:S(2)}) async-start(f32[2,32,8,8192]{3,2,0,1:T(8,128)} %pad_maximum_fusion), calls=%async_computation.2 | async-start | bytes 33554432 | tf_op jit(solution)/shard_map/all_to_all | solution.py:121
  572.9 97.6 %all-to-all-start.3 = ((bf16[2,2,128,4096]{3,0,1,2:T(2,128)(2,1)}), bf16[2,2,128,4096]{3,0,1,2:T(2,128)(2,1)}, u32[]{:S(2)}, u32[]{:S(2)}) async-start(bf16[2,2,128,4096]{3,0,1,2:T(2,128)(2,1)} %copy.59), calls=%async_computation.3 | async-start | bytes 8388608 | tf_op jit(solution)/shard_map/all_to_all | solution.py:126
  680.5 33.6 %copy-start.2 = (f32[4096]{0:T(1024)S(1)}, f32[4096]{0:T(1024)}, u32[]{:S(2)}) copy-start(f32[4096]{0:T(1024)} %param.11) | copy-start | bytes 49156
  682.1 32.0 %all-to-all-start.4 = ((bf16[16,8,4096]{2,1,0:T(8,128)(2,1)}), bf16[16,8,4096]{2,1,0:T(8,128)(2,1)}, u32[]{:S(2)}, u32[]{:S(2)}) async-start(bf16[16,8,4096]{2,1,0:T(8,128)(2,1)} %bitcast.79), calls=%async_computation.4 | async-start | bytes 2097152 | tf_op jit(solution)/shard_map/all_to_all | solution.py:130
